TPU v7x, 32 devices: a whole 2x2x4 slice. The times are simulated.
32 devices in a mesh: grp: 4 (over z), blk: 8 (over y, x, core).
Axes of the slice: x: 2, y: 2, z: 4, core: 2. Of those that a mesh axis runs over, the one named last changes fastest.
Arguments:
- tokens: bfloat16 [8192, 2048], P(('grp', 'blk')), may hold values from -9 to 9
- block_group: int32 [64], replicated, may hold values from 0 to 3, as said below
- block_slot: int32 [64], replicated, may hold values from 0 to 15, as said below
- attn_gain: bfloat16 [2048], P(('grp', 'blk')), may hold values from 0.5 to 1.5
- w_query: bfloat16 [2048, 2048], P(('grp', 'blk')), may hold values from -0.5 to 0.5
- w_key: bfloat16 [2048, 512], P(('grp', 'blk')), may hold values from -0.5 to 0.5
- w_value: bfloat16 [2048, 512], P(('grp', 'blk')), may hold values from -0.125 to 0.125
- w_out: bfloat16 [2048, 2048], P(('grp', 'blk')), may hold values from -2 to 2
- mlp_gain: bfloat16 [2048], P(('grp', 'blk')), may hold values from 0.5 to 1.5
- w_gate: bfloat16 [2048, 8192], P(None, ('grp', 'blk')), may hold values from -0.125 to 0.125
- w_up: bfloat16 [2048, 8192], P(None, ('grp', 'blk')), may hold values from -0.125 to 0.125
- w_down: bfloat16 [8192, 2048], P(('grp', 'blk')), may hold values from -0.5 to 0.5
- cotangent: bfloat16 [8192, 2048], P(('grp', 'blk')), may hold values from -6 to 6
Outputs:
- output: bfloat16 [8192, 2048], P(('grp', 'blk'))
- tokens_grad: bfloat16 [8192, 2048], P(('grp', 'blk'))
- attn_gain_grad: float32 [2048], P(('grp', 'blk'))
- w_query_grad: float32 [2048, 2048], P(('grp', 'blk'))
- w_key_grad: float32 [2048, 512], P(('grp', 'blk'))
- w_value_grad: float32 [2048, 512], P(('grp', 'blk'))
- w_out_grad: float32 [2048, 2048], P(('grp', 'blk'))
- mlp_gain_grad: float32 [2048], P(('grp', 'blk'))
- w_gate_grad: float32 [2048, 8192], P(None, ('grp', 'blk'))
- w_up_grad: float32 [2048, 8192], P(None, ('grp', 'blk'))
- w_down_grad: float32 [8192, 2048], P(('grp', 'blk'))
- rms_stats: float32 [3], replicated
Inputs may be any that keep to these rules, and one draw needn't show every extreme that they name: `block_group`: each group has 16 blocks, one of each slot, and all of them lie in one aligned run of 16 blocks. `block_slot`: slots below 8 are the prompt's parts in order, the others its continuations.
All inputs are finite; a program needn't handle non-finite values.
Results may differ from a plain program's by a relative error of at most 0.019.
Values may be sent and summed in bfloat16 or wider, within the bound.
A program may use at most 448 MiB of HBM per device.

v0:
```python
import jax
import jax.numpy as jnp
from jax import lax
from jax.sharding import Mesh
from jax.sharding import PartitionSpec as P

D = 2048
HEADS = 32
KV_HEADS = 8
HEAD_DIM = 64
BLOCK = 128
PROMPT_BLOCKS = 8
GROUP_BLOCKS = 16
PER_GROUP = HEADS // KV_HEADS
ATTN_MULT = 0.015625
RESID_MULT = 0.22
EPSILON = 1e-05
MASKED = -1e30
PLANE = ("chip", "core")
EVERY = ("grp", "chip", "core")
BF16 = jnp.bfloat16
F32 = jnp.float32


def matmul(left, right):
    return jnp.dot(left, right, preferred_element_type=F32)


def over_rows(left, right):
    return lax.dot_general(left, right, (((0,), (0,)), ((), ())), preferred_element_type=F32)


def over_cols(left, right):
    return lax.dot_general(left, right, (((1,), (1,)), ((), ())), preferred_element_type=F32)


def gather(values, axes, axis=0):
    return lax.all_gather(values, axes, axis=axis, tiled=True)


def scatter(values, axes, axis=0):
    return lax.psum_scatter(values, axes, scatter_dimension=axis, tiled=True)


def norm_parts(values):
    factor = lax.rsqrt(jnp.mean(values * values, axis=-1, keepdims=True) + EPSILON)
    return factor


def norm_back(values, factor, gain, grad):
    scaled = gain * grad
    inner = jnp.mean(values * scaled, axis=-1, keepdims=True)
    return (
        factor * scaled - values * (factor * factor * factor * inner),
        jnp.sum(grad * values * factor, axis=0),
    )


def on_device(
    tokens,
    block_group,
    block_slot,
    attn_gain,
    w_query,
    w_key,
    w_value,
    w_out,
    mlp_gain,
    w_gate,
    w_up,
    w_down,
    cotangent,
):
    tok_axes, weight_axes = (TOK_AXES, WEIGHT_AXES)
    grps = lax.axis_size("grp")
    devs = lax.axis_size(PLANE)
    rows = tokens.shape[0]
    w_rows = w_query.shape[0]
    q_heads = HEADS // devs
    kv_heads = max(1, KV_HEADS // devs)
    kv_copies = max(1, devs // KV_HEADS)
    q_cols, kv_cols = (q_heads * HEAD_DIM, kv_heads * HEAD_DIM)
    row_blocks = rows // BLOCK * devs
    row_groups = row_blocks // GROUP_BLOCKS
    row_first = lax.axis_index("grp") * row_blocks
    keys = lax.dynamic_slice_in_dim(block_group, row_first, row_blocks) * GROUP_BLOCKS
    keys = keys + lax.dynamic_slice_in_dim(block_slot, row_first, row_blocks)
    rank = jnp.sum((keys[None, :] < keys[:, None]).astype(jnp.int32), axis=1)
    ids = jnp.arange(row_blocks, dtype=jnp.int32)
    order = jnp.sum(jnp.where(rank[None, :] == ids[:, None], ids[None, :], 0), axis=1)

    def kv_split(w):
        w = w.reshape(w_rows, devs // kv_copies, kv_cols)
        return jnp.repeat(w, kv_copies, axis=1) if kv_copies > 1 else w

    gains = jnp.stack([attn_gain, mlp_gain], axis=1)
    gains = jnp.broadcast_to(jnp.pad(gains, ((0, 0), (0, 126)))[:, None, :], (w_rows, devs, 128))
    packed = jnp.concatenate(
        [w_query.reshape(w_rows, devs, q_cols), kv_split(w_key), kv_split(w_value), gains], axis=2
    )
    packed = lax.all_to_all(packed, PLANE, split_axis=1, concat_axis=0, tiled=True)
    packed = gather(packed.reshape(devs * w_rows, q_cols + 2 * kv_cols + 128), "grp")
    w_qkv = packed[:, : q_cols + 2 * kv_cols]
    gain_one = packed[:, q_cols + 2 * kv_cols].astype(F32)
    gain_two = packed[:, q_cols + 2 * kv_cols + 1].astype(F32)
    all_tokens = gather(tokens, PLANE)
    layer_all = all_tokens.astype(F32)
    normed_one = (layer_all * norm_parts(layer_all) * gain_one).astype(BF16)
    qkv = matmul(normed_one, w_qkv).astype(BF16)
    qkv = qkv.reshape(row_blocks, BLOCK, q_cols + 2 * kv_cols)[order]
    qkv = qkv.reshape(row_groups, GROUP_BLOCKS * BLOCK, q_cols + 2 * kv_cols)
    seq = GROUP_BLOCKS * BLOCK
    per_kv = q_heads // kv_heads
    q = qkv[:, :, :q_cols].reshape(row_groups, seq, kv_heads, per_kv, HEAD_DIM)
    k = qkv[:, :, q_cols : q_cols + kv_cols].reshape(row_groups, seq, kv_heads, HEAD_DIM)
    v = qkv[:, :, q_cols + kv_cols :].reshape(row_groups, seq, kv_heads, HEAD_DIM)
    prompt = PROMPT_BLOCKS * BLOCK
    row_id = jnp.arange(seq)
    q_b = q.reshape(row_groups, GROUP_BLOCKS, BLOCK, kv_heads, per_kv, HEAD_DIM)
    k_b = k.reshape(row_groups, GROUP_BLOCKS, BLOCK, kv_heads, HEAD_DIM)
    v_b = v.reshape(row_groups, GROUP_BLOCKS, BLOCK, kv_heads, HEAD_DIM)
    k_p, v_p = (k[:, :prompt], v[:, :prompt])
    starts = jnp.minimum(jnp.arange(GROUP_BLOCKS), PROMPT_BLOCKS) * BLOCK
    see_p = jnp.arange(prompt)[None, :] < starts[:, None]
    see_o = jnp.arange(BLOCK)[None, :] <= jnp.arange(BLOCK)[:, None]

    def all_scores():
        far = jnp.einsum("gbikpd,gjkd->gbkpij", q_b, k_p, preferred_element_type=F32)
        far = jnp.where(see_p[None, :, None, None, None, :], far * ATTN_MULT, MASKED)
        own = jnp.einsum("gbikpd,gbjkd->gbkpij", q_b, k_b, preferred_element_type=F32)
        own = jnp.where(see_o[None, None, None, None, :, :], own * ATTN_MULT, MASKED)
        return (far, own)

    far, own = all_scores()
    peak = jnp.maximum(far.max(-1, keepdims=True), own.max(-1, keepdims=True))
    far, own = (jnp.exp(far - peak), jnp.exp(own - peak))
    total = far.sum(-1, keepdims=True) + own.sum(-1, keepdims=True)
    far_p, own_p = (far / total, own / total)
    attended = jnp.einsum(
        "gbkpij,gjkd->gbikpd", far_p.astype(BF16), v_p, preferred_element_type=F32
    ) + jnp.einsum("gbkpij,gbjkd->gbikpd", own_p.astype(BF16), v_b, preferred_element_type=F32)
    attended = attended.astype(BF16).reshape(row_blocks, BLOCK, q_cols)[rank]
    attended = lax.all_to_all(
        attended.reshape(row_blocks * BLOCK, q_cols), PLANE, split_axis=0, concat_axis=1, tiled=True
    )
    out_full = gather(w_out, EVERY)
    layer_in = tokens.astype(F32)
    branch_attn = matmul(attended, out_full)
    residual = layer_in + RESID_MULT * branch_attn
    factor_two = norm_parts(residual)
    normed_two = gather((residual * factor_two * gain_two).astype(BF16), tok_axes)
    upstream = cotangent.astype(F32)
    d_branch_mlp = gather((RESID_MULT * upstream).astype(BF16), tok_axes)
    gate_w = gather(w_gate, weight_axes, axis=1)
    up_w = gather(w_up, weight_axes, axis=1)
    down_w = gather(w_down, weight_axes)
    gate_act = matmul(normed_two, gate_w)
    up_act = matmul(normed_two, up_w)
    sig = jax.nn.sigmoid(gate_act)
    silu = gate_act * sig
    hidden = (silu * up_act).astype(BF16)
    branch_mlp = scatter(matmul(hidden, down_w).astype(BF16), tok_axes).astype(F32)
    layer_out = residual + RESID_MULT * branch_mlp
    grad_down = scatter(over_rows(hidden, d_branch_mlp).astype(BF16), weight_axes).astype(F32)
    d_hidden = over_cols(d_branch_mlp, down_w)
    d_gate = (d_hidden * up_act * (sig * (1.0 + gate_act * (1.0 - sig)))).astype(BF16)
    d_up = (d_hidden * silu).astype(BF16)
    grad_gate = scatter(over_rows(normed_two, d_gate).astype(BF16), weight_axes, axis=1).astype(F32)
    grad_up = scatter(over_rows(normed_two, d_up).astype(BF16), weight_axes, axis=1).astype(F32)
    d_normed_two = over_cols(d_gate, gate_w) + over_cols(d_up, up_w)
    d_normed_two = scatter(d_normed_two.astype(BF16), tok_axes).astype(F32)
    d_residual_norm, d_gain_two = norm_back(residual, factor_two, gain_two, d_normed_two)
    d_residual = upstream + d_residual_norm
    d_branch_attn = (RESID_MULT * d_residual).astype(BF16)
    grad_out = scatter(over_rows(attended, d_branch_attn).astype(BF16), EVERY).astype(F32)
    d_attended = over_cols(d_branch_attn, out_full).astype(BF16)
    d_attended = lax.all_to_all(d_attended, PLANE, split_axis=1, concat_axis=0, tiled=True)
    d_b = d_attended.reshape(row_blocks, BLOCK, q_cols)[order]
    d_b = d_b.reshape(row_groups, GROUP_BLOCKS, BLOCK, kv_heads, per_kv, HEAD_DIM)
    far_s = jnp.einsum("gbikpd,gjkd->gbkpij", d_b, v_p, preferred_element_type=F32)
    own_s = jnp.einsum("gbikpd,gbjkd->gbkpij", d_b, v_b, preferred_element_type=F32)
    mean_s = (far_p * far_s).sum(-1, keepdims=True) + (own_p * own_s).sum(-1, keepdims=True)
    far_d = (far_p * (far_s - mean_s)).astype(BF16)
    own_d = (own_p * (own_s - mean_s)).astype(BF16)
    far_p, own_p = (far_p.astype(BF16), own_p.astype(BF16))
    d_q = ATTN_MULT * (
        jnp.einsum("gbkpij,gjkd->gbikpd", far_d, k_p, preferred_element_type=F32)
        + jnp.einsum("gbkpij,gbjkd->gbikpd", own_d, k_b, preferred_element_type=F32)
    )
    d_k = jnp.einsum("gbkpij,gbikpd->gbjkd", own_d, q_b, preferred_element_type=F32)
    d_v = jnp.einsum("gbkpij,gbikpd->gbjkd", own_p, d_b, preferred_element_type=F32)
    d_kp = jnp.einsum("gbkpij,gbikpd->gjkd", far_d, q_b, preferred_element_type=F32)
    d_vp = jnp.einsum("gbkpij,gbikpd->gjkd", far_p, d_b, preferred_element_type=F32)
    d_k = ATTN_MULT * jnp.concatenate(
        [
            d_k.reshape(row_groups, seq, kv_cols)[:, :prompt]
            + d_kp.reshape(row_groups, prompt, kv_cols),
            d_k.reshape(row_groups, seq, kv_cols)[:, prompt:],
        ],
        axis=1,
    )
    d_v = jnp.concatenate(
        [
            d_v.reshape(row_groups, seq, kv_cols)[:, :prompt]
            + d_vp.reshape(row_groups, prompt, kv_cols),
            d_v.reshape(row_groups, seq, kv_cols)[:, prompt:],
        ],
        axis=1,
    )
    d_qkv = jnp.concatenate([d_q.reshape(row_groups, seq, q_cols), d_k, d_v], axis=2).astype(BF16)
    d_qkv = d_qkv.reshape(row_blocks, BLOCK, q_cols + 2 * kv_cols)[rank]
    d_qkv = d_qkv.reshape(row_blocks * BLOCK, q_cols + 2 * kv_cols)
    d_normed_one = scatter(over_cols(d_qkv, w_qkv).astype(BF16), PLANE).astype(F32)
    d_input_norm, d_gain_one = norm_back(layer_in, norm_parts(layer_in), gain_one, d_normed_one)
    tokens_grad = (d_residual + d_input_norm).astype(BF16)
    grad_qkv = over_rows(normed_one, d_qkv)
    d_gains = jnp.pad(jnp.stack([d_gain_one, d_gain_two], axis=1), ((0, 0), (0, 126)))
    sent = scatter(jnp.concatenate([grad_qkv, d_gains], axis=1).astype(BF16), "grp")
    sent = sent.reshape(devs, w_rows, q_cols + 2 * kv_cols + 128)
    sent = lax.all_to_all(sent, PLANE, split_axis=0, concat_axis=0, tiled=True).astype(F32)

    def kv_join(g):
        g = g.reshape(devs // kv_copies, kv_copies, w_rows, kv_cols)
        g = jnp.sum(g, axis=1) if kv_copies > 1 else g[:, 0]
        return jnp.swapaxes(g, 0, 1).reshape(w_rows, KV_HEADS * HEAD_DIM)

    grad_query = jnp.swapaxes(sent[:, :, :q_cols], 0, 1).reshape(w_rows, D)
    grad_key = kv_join(sent[:, :, q_cols : q_cols + kv_cols])
    grad_value = kv_join(sent[:, :, q_cols + kv_cols : q_cols + 2 * kv_cols])
    gains_sum = jnp.sum(sent[:, :, q_cols + 2 * kv_cols :], axis=0)
    scaled_attn = RESID_MULT * branch_attn
    scaled_mlp = RESID_MULT * branch_mlp
    squares = jnp.stack(
        [
            jnp.sum(layer_out * layer_out),
            jnp.sum(scaled_attn * scaled_attn),
            jnp.sum(scaled_mlp * scaled_mlp),
        ]
    )
    totals = lax.psum(squares, EVERY)
    rms_stats = jnp.sqrt(totals / (rows * grps * devs * D))
    return (
        layer_out.astype(BF16),
        tokens_grad,
        gains_sum[:, 0],
        grad_query,
        grad_key,
        grad_value,
        grad_out,
        gains_sum[:, 1],
        grad_gate,
        grad_up,
        grad_down,
        rms_stats,
    )


TOK_AXES, WEIGHT_AXES = (PLANE, ("grp",))


def solution(mesh):
    shape = (mesh.shape["grp"], mesh.shape["blk"] // 2, 2)
    mesh = Mesh(mesh.devices.reshape(shape), EVERY)
    row, col, vec = (P(EVERY, None), P(None, EVERY), P(EVERY))
    return jax.shard_map(
        on_device,
        mesh=mesh,
        in_specs=(row, P(), P(), vec, row, row, row, row, vec, col, col, row, row),
        out_specs=(row, row, vec, row, row, row, row, vec, col, col, row, P()),
        check_vma=False,
    )
```

profile of v0, /device:TPU:0, one launch (start us, length us, event | category | flops | bytes accessed | tf_op | source)
XLA Modules:
  0.0 1417.4 jit_solution(8293760625746567301)
XLA Ops:
  11.4 14.8 %all_to_all.55 = bf16[64,8,512]{2,0,1:T(8,128)(2,1)} all-to-all(bf16[64,8,512]{2,0,1:T(8,128)(2,1)S(1)} %copy.186), channel_id=1, replica_groups=mesh['grp'=4,'chip'=4,'core'=2] {'chip','core'}, dimensions={1} | all-to-all | bytes 1048576 | tf_op jit(solution)/shard_map/all_to_all | solution.py:101
  28.9 42.7 %all-gather.11.cloned.1.call-done = bf16[2048,512]{1,0:T(8,128)(2,1)} async-done(((bf16[512,512]{1,0:T(8,128)(2,1)}), bf16[2048,512]{1,0:T(8,128)(2,1)}) %all-gather.11.cloned.1.call-update) | async-done | bytes 2097168 | tf_op jit(solution)/shard_map/all_gather | solution.py:38
  73.5 53.2 %all-gather.9.cloned.1.call-done = bf16[2048,2048]{1,0:T(8,128)(2,1)} async-done(((bf16[256,2048]{1,0:T(8,128)(2,1)}), bf16[2048,2048]{1,0:T(8,128)(2,1)}) %all-gather.9.cloned.1.call-update) | async-done | bytes 8388624 | tf_op jit(solution)/shard_map/all_gather | solution.py:38
  173.9 15.7 %fusion.42 = bf16[1,16,128,1,4,64]{2,5,4,1,3,0:T(8,128)(2,1)S(1)} fusion(f32[16,64,4,128]{3,1,2,0:T(8,128)S(1)} %fusion.45, bf16[1,2048,1,64]{1,3,2,0:T(8,128)(2,1)S(1)} %bitcast.311, f32[16,4,128]{2,1,0:T(4,128)S(1)} %add.138, f32[16,4,128]{2,1,0:T(4,128)S(1)} %max.8, f32[1024,16,128,4]{2,0,3,1:T(8,128)} %copy-done, ...), kind=kOutput, calls=%fused_computation.82 | convolution fusion | flops 1116733440 | bytes 36913152 | tf_op jit(solution)/shard_map/gbkpij,gjkd->gbikpd/dot_general | solution.py:139
  190.8 18.6 %all_to_all.56 = bf16[8,256,256]{2,1,0:T(8,128)(2,1)S(1)} all-to-all(bf16[8,256,256]{2,1,0:T(8,128)(2,1)S(1)} %bitcast.291), channel_id=1, replica_groups=mesh['grp'=4,'chip'=4,'core'=2] {'chip','core'}, dimensions={0} | all-to-all | bytes 2097152 | tf_op jit(solution)/shard_map/all_to_all | solution.py:143
  222.2 65.5 %all-gather.19.cloned.1.call-done = bf16[2048,1024]{1,0:T(8,128)(2,1)} async-done(((bf16[2048,256]{1,0:T(8,128)(2,1)}), bf16[2048,1024]{1,0:T(8,128)(2,1)}) %all-gather.19.cloned.1.call-update) | async-done | bytes 4194320 | tf_op jit(solution)/shard_map/all_gather | solution.py:38
  287.7 54.9 %all-gather.15.cloned.1.call-done = bf16[2048,2048]{1,0:T(8,128)(2,1)} async-done(((bf16[256,2048]{1,0:T(8,128)(2,1)}), bf16[2048,2048]{1,0:T(8,128)(2,1)}) %all-gather.15.cloned.1.call-update) | async-done | bytes 8388624 | tf_op jit(solution)/shard_map/all_gather | solution.py:38
  342.6 14.8 %fusion.94 = f32[2048,1024]{1,0:T(8,128)} fusion(bf16[2048,2048]{1,0:T(8,128)(2,1)} %all-gather.15.cloned.1.call-done, bf16[2048,1024]{1,0:T(8,128)(2,1)} %all-gather.19.cloned.1.call-done), kind=kOutput, calls=%fused_computation.166 | convolution fusion | flops 8589934592 | bytes 20971520 | tf_op jit(solution)/shard_map/dot_general | solution.py:26
  357.4 67.2 %all-gather.17.cloned.1.call-done = bf16[2048,1024]{1,0:T(8,128)(2,1)} async-done(((bf16[2048,256]{1,0:T(8,128)(2,1)}), bf16[2048,1024]{1,0:T(8,128)(2,1)}) %all-gather.17.cloned.1.call-update) | async-done | bytes 4194320 | tf_op jit(solution)/shard_map/all_gather | solution.py:38
  424.6 14.4 %fusion.93 = f32[2048,1024]{1,0:T(8,128)} fusion(bf16[2048,2048]{1,0:T(8,128)(2,1)} %all-gather.15.cloned.1.call-done, bf16[2048,1024]{1,0:T(8,128)(2,1)} %all-gather.17.cloned.1.call-done), kind=kOutput, calls=%fused_computation.165 | convolution fusion | flops 8589934592 | bytes 20971520 | tf_op jit(solution)/shard_map/dot_general | solution.py:26
  439.0 66.2 %all-gather.21.cloned.1.call-done = bf16[1024,2048]{1,0:T(8,128)(2,1)} async-done(((bf16[256,2048]{1,0:T(8,128)(2,1)}), bf16[1024,2048]{1,0:T(8,128)(2,1)}) %all-gather.21.cloned.1.call-update) | async-done | bytes 4194320 | tf_op jit(solution)/shard_map/all_gather | solution.py:38
  505.2 55.4 %all-gather.23.cloned.1.call-done = bf16[2048,2048]{1,0:T(8,128)(2,1)} async-done(((bf16[256,2048]{1,0:T(8,128)(2,1)}), bf16[2048,2048]{1,0:T(8,128)(2,1)}) %all-gather.23.cloned.1.call-update) | async-done | bytes 8388624 | tf_op jit(solution)/shard_map/all_gather | solution.py:38
  560.6 23.2 %multiply_convert_fusion = (bf16[2048,1024]{1,0:T(8,128)(2,1)}, bf16[2048,1024]{1,0:T(8,128)(2,1)}, bf16[2048,1024]{1,0:T(8,128)(2,1)}) fusion(f32[2048,1024]{1,0:T(8,128)} %fusion.93, f32[2048,1024]{1,0:T(8,128)} %fusion.94, bf16[2048,2048]{1,0:T(8,128)(2,1)} %all-gather.23.cloned.1.call-done, bf16[1024,2048]{1,0:T(8,128)(2,1)} %all-gather.21.cloned.1.call-done), kind=kOutput, calls=%fused_computation.26 | convolution fusion | flops 8621391872 | bytes 41943040 | tf_op jit(solution)/shard_map/dot_general | solution.py:34
  583.8 13.9 convolution_convert_fusion.2
  597.8 16.3 %fusion.95 = f32[2048,2048]{1,0:T(8,128)} fusion(bf16[2048,1024]{1,0:T(8,128)(2,1)} %get-tuple-element.24, bf16[2048,1024]{1,0:T(8,128)(2,1)} %all-gather.17.cloned.1.call-done), kind=kOutput, calls=%fused_computation.167 | convolution fusion | flops 8589934592 | bytes 25165824 | tf_op jit(solution)/shard_map/dot_general | solution.py:34
  614.1 16.1 %add_convert_fusion = bf16[2048,2048]{1,0:T(8,128)(2,1)} fusion(f32[2048,2048]{1,0:T(8,128)} %fusion.95, bf16[2048,1024]{1,0:T(8,128)(2,1)} %get-tuple-element.23, bf16[2048,1024]{1,0:T(8,128)(2,1)S(1)} %copy-done.41), kind=kOutput, calls=%fused_computation.24 | convolution fusion | flops 8598323200 | bytes 33554432 | tf_op jit(solution)/shard_map/dot_general | solution.py:34
  630.5 38.7 %reduce-scatter.9.cloned.1.call-done = bf16[256,2048]{1,0:T(8,128)(2,1)} async-done(((bf16[2048,2048]{1,0:T(8,128)(2,1)}), bf16[256,2048]{1,0:T(8,128)(2,1)}) %reduce-scatter.9.cloned.1.call-update) | async-done | bytes 1048592 | tf_op jit(solution)/shard_map/reduce_scatter | solution.py:42
  669.1 75.0 %reduce-scatter.11.cloned.1.call-done = bf16[256,2048]{1,0:T(8,128)(2,1)} async-done(((bf16[2048,2048]{1,0:T(8,128)(2,1)}), bf16[256,2048]{1,0:T(8,128)(2,1)}) %reduce-scatter.11.cloned.1.call-update) | async-done | bytes 1048592 | tf_op jit(solution)/shard_map/reduce_scatter | solution.py:42
  755.8 17.9 %all_to_all.57 = bf16[256,8,256]{2,0,1:T(8,128)(2,1)S(1)} all-to-all(bf16[256,8,256]{2,0,1:T(8,128)(2,1)S(1)} %bitcast.293), channel_id=1, replica_groups=mesh['grp'=4,'chip'=4,'core'=2] {'chip','core'}, dimensions={1} | all-to-all | bytes 2097152 | tf_op jit(solution)/shard_map/all_to_all | solution.py:177
  782.6 26.2 %fusion = (f32[16,4,128]{2,1,0:T(4,128)S(1)}, f32[1024,16,128,4]{2,0,3,1:T(8,128)}) fusion(f32[16,4,128]{2,1,0:T(4,128)S(1)} %copy-done.26, f32[16,4,128]{2,1,0:T(4,128)S(1)} %copy-done.22, f32[1024,16,128,4]{2,0,3,1:T(8,128)} %copy-done, pred[16,1024]{1,0:T(8,128)(4,1)S(1)} %copy-done.24, bf16[16,128,4,64]{1,3,2,0:T(8,128)(2,1)S(1)} %bitcast.316, ...), kind=kOutput, calls=%fused_computation.7 | convolution fusion | flops 1124065280 | bytes 68403200 | tf_op jit(solution)/shard_map/gbikpd,gjkd->gbkpij/dot_general | solution.py:180
  808.8 14.7 %fusion.65 = bf16[1,1024,64]{1,2,0:T(8,128)(2,1)S(1)} fusion(bf16[16,128,4,64]{1,3,2,0:T(8,128)(2,1)S(1)} %bitcast.317, f32[1,1024,64]{1,0,2:T(1,128)S(1)} %slice.91, f32[16,4,128]{2,1,0:T(4,128)S(1)} %copy-done.26, f32[16,4,128]{2,1,0:T(4,128)S(1)} %copy-done.22, f32[1024,16,128,4]{2,0,3,1:T(8,128)} %copy-done, pred[16,1024]{1,0:T(8,128)(4,1)S(1)} %copy-done.24), kind=kOutput, calls=%fused_computation.107 | convolution fusion | flops 1115815936 | bytes 35078144 | tf_op jit(solution)/shard_map/gbkpij,gbikpd->gjkd/dot_general | solution.py:193
  823.8 28.1 %fusion.9 = bf16[16,4,128,1024]{2,3,1,0:T(8,128)(2,1)} fusion(f32[1024,16,128,4]{2,0,3,1:T(8,128)} %get-tuple-element.41, f32[16,4,128]{2,1,0:T(4,128)S(1)} %add.149, f32[16,4,128]{2,1,0:T(4,128)S(1)} %copy-done.26, f32[16,4,128]{2,1,0:T(4,128)S(1)} %copy-done.22, f32[1024,16,128,4]{2,0,3,1:T(8,128)} %copy-done, pred[16,1024]{1,0:T(8,128)(4,1)S(1)} %copy-done.24), kind=kLoop, calls=%fused_computation.19 | loop fusion | flops 58720256 | bytes 84000768 | tf_op jit(solution)/shard_map/reshape.53
  869.0 10.9 fusion.61
  897.8 14.3 %convolution_convert_fusion.3 = bf16[1024,2048]{1,0:T(8,128)(2,1)} fusion(bf16[2048,1024]{1,0:T(8,128)(2,1)} %get-tuple-element.25, bf16[2048,2048]{1,0:T(8,128)(2,1)} %all-gather.23.cloned.1.call-done), kind=kOutput, calls=%fused_computation.46 | convolution fusion | flops 8592031744 | bytes 16777216 | tf_op jit(solution)/shard_map/dot_general | solution.py:30
  912.2 14.3 %convolution_convert_fusion.4 = bf16[2048,1024]{1,0:T(8,128)(2,1)} fusion(bf16[2048,2048]{1,0:T(8,128)(2,1)} %all-gather.15.cloned.1.call-done, bf16[2048,1024]{1,0:T(8,128)(2,1)} %get-tuple-element.23), kind=kOutput, calls=%fused_computation.47 | convolution fusion | flops 8592031744 | bytes 16777216 | tf_op jit(solution)/shard_map/dot_general | solution.py:30
  926.5 14.5 %convolution_convert_fusion.5 = bf16[2048,1024]{1,0:T(8,128)(2,1)} fusion(bf16[2048,2048]{1,0:T(8,128)(2,1)} %all-gather.15.cloned.1.call-done, bf16[2048,1024]{1,0:T(8,128)(2,1)} %get-tuple-element.24), kind=kOutput, calls=%fused_computation.48 | convolution fusion | flops 8592031744 | bytes 16777216 | tf_op jit(solution)/shard_map/dot_general | solution.py:30
  951.1 17.2 %reduce-scatter.13.cloned.1.call-done = bf16[256,2048]{1,0:T(8,128)(2,1)} async-done(((bf16[2048,2048]{1,0:T(8,128)(2,1)}), bf16[256,2048]{1,0:T(8,128)(2,1)}) %reduce-scatter.13.cloned.1.call-update) | async-done | bytes 1048592 | tf_op jit(solution)/shard_map/reduce_scatter | solution.py:42
  980.5 66.9 %reduce-scatter.23.cloned.1.call-done = bf16[256,2048]{1,0:T(8,128)(2,1)} async-done(((bf16[1024,2048]{1,0:T(8,128)(2,1)}), bf16[256,2048]{1,0:T(8,128)(2,1)}) %reduce-scatter.23.cloned.1.call-update) | async-done | bytes 1048592 | tf_op jit(solution)/shard_map/reduce_scatter | solution.py:42
  1050.1 76.8 %reduce-scatter.21.cloned.1.call-done = bf16[2048,256]{1,0:T(8,128)(2,1)} async-done(((bf16[2048,1024]{1,0:T(8,128)(2,1)}), bf16[2048,256]{1,0:T(8,128)(2,1)}) %reduce-scatter.21.cloned.1.call-update) | async-done | bytes 1048592 | tf_op jit(solution)/shard_map/reduce_scatter | solution.py:42
  1131.7 74.8 %reduce-scatter.19.cloned.1.call-done = bf16[2048,256]{1,0:T(8,128)(2,1)} async-done(((bf16[2048,1024]{1,0:T(8,128)(2,1)}), bf16[2048,256]{1,0:T(8,128)(2,1)}) %reduce-scatter.19.cloned.1.call-update) | async-done | bytes 1048592 | tf_op jit(solution)/shard_map/reduce_scatter | solution.py:42
  1209.2 44.4 %psum.7 = f32[3]{0:T(128)S(1)} all-reduce(f32[3]{0:T(128)S(1)} %pad_maximum_fusion.5), channel_id=1, replica_groups=mesh['grp'=4,'chip'=4,'core'=2] {'grp','chip','core'}, use_global_device_ids=true, to_apply=%region_27.28 | all-reduce | flops 3 | bytes 24 | tf_op jit(solution)/shard_map/psum | solution.py:240
  1263.1 140.9 %reduce-scatter.17.cloned.1.call-done = bf16[64,2048]{1,0:T(8,128)(2,1)} async-done(((bf16[2048,2048]{1,0:T(8,128)(2,1)}), bf16[64,2048]{1,0:T(8,128)(2,1)}) %reduce-scatter.17.cloned.1.call-update) | async-done | bytes 262160 | tf_op jit(solution)/shard_map/reduce_scatter | solution.py:42
  (222 shorter events, 173.7 us)
Async XLA Ops:
  7.2 21.2 %copy-start.39 = (s32[64]{0:T(128)S(1)}, s32[64]{0:T(128)}, u32[]{:S(2)}) copy-start(s32[64]{0:T(128)} %param.15) | copy-start | bytes 772
  7.2 21.2 %copy-start.40 = (s32[64]{0:T(128)S(1)}, s32[64]{0:T(128)}, u32[]{:S(2)}) copy-start(s32[64]{0:T(128)} %param.14) | copy-start | bytes 772
  7.2 64.5 %all-gather.11.cloned.1.call-start = ((), (), s32[]{:S(2)}) async-start(), calls=%async_computation.13 | async-start | bytes 2621440 | tf_op jit(solution)/shard_map/all_gather | solution.py:38
  26.2 100.5 %all-gather.9.cloned.1.call-start = ((), (), s32[]{:S(2)}) async-start(), calls=%async_computation.12 | async-start | bytes 9437184 | tf_op jit(solution)/shard_map/all_gather | solution.py:38
  27.0 183.8 %all-gather.13.cloned.1.call-start = ((), (), s32[]{:S(2)}) async-start(), calls=%async_computation.14 | async-start | bytes 8650752 | tf_op jit(solution)/shard_map/all_gather | solution.py:38
  27.7 260.0 %all-gather.19.cloned.1.call-start = ((), (), s32[]{:S(2)}) async-start(), calls=%async_computation.17 | async-start | bytes 5242880 | tf_op jit(solution)/shard_map/all_gather | solution.py:38
  28.3 314.3 %all-gather.15.cloned.1.call-start = ((), (), s32[]{:S(2)}) async-start(), calls=%async_computation.15 | async-start | bytes 9437184 | tf_op jit(solution)/shard_map/all_gather | solution.py:38
  28.8 143.8 %copy-start.29 = (pred[128,128]{0,1:T(8,128)(4,1)}, pred[128,128]{0,1:T(8,128)(4,1)S(1)}, u32[]{:S(2)}) copy-start(pred[128,128]{0,1:T(8,128)(4,1)S(1)} %iota_compare_fusion.1) | copy-start | bytes 49156
  28.8 109.9 %copy-start.38 = (s32[1024]{0:T(1024)}, s32[1024]{0:T(1024)S(1)}, u32[]{:S(2)}) copy-start(s32[1024]{0:T(1024)S(1)} %pad_clamp_fusion.1) | copy-start | bytes 12292
  28.8 161.3 %copy-start.37 = (s32[1024]{0:T(1024)}, s32[1024]{0:T(1024)S(1)}, u32[]{:S(2)}) copy-start(s32[1024]{0:T(1024)S(1)} %pad_clamp_fusion) | copy-start | bytes 12292
  28.9 144.9 %copy-start.23 = (pred[16,1024]{1,0:T(8,128)(4,1)}, pred[16,1024]{1,0:T(8,128)(4,1)S(1)}, u32[]{:S(2)}) copy-start(pred[16,1024]{1,0:T(8,128)(4,1)S(1)} %iota_compare_fusion.2) | copy-start | bytes 49156
  73.5 58.5 %copy-start.31 = (f32[2048]{0:T(1024)}, f32[2048]{0:T(1024)S(1)}, u32[]{:S(2)}) copy-start(f32[2048]{0:T(1024)S(1)} %get-tuple-element.18) | copy-start | bytes 24580
  156.8 17.1 %copy-start.21 = (f32[16,4,128]{2,1,0:T(4,128)}, f32[16,4,128]{2,1,0:T(4,128)S(1)}, u32[]{:S(2)}) copy-start(f32[16,4,128]{2,1,0:T(4,128)S(1)} %max.8) | copy-start | bytes 98308
  189.6 21.1 %copy-start.7 = (bf16[256,2048]{1,0:T(8,128)(2,1)S(1)}, bf16[256,2048]{1,0:T(8,128)(2,1)}, u32[]{:S(2)}) copy-start(bf16[256,2048]{1,0:T(8,128)(2,1)} %param.13) | copy-start | bytes 3145732
  219.5 205.1 %all-gather.17.cloned.1.call-start = ((), (), s32[]{:S(2)}) async-start(), calls=%async_computation.16 | async-start | bytes 5242880 | tf_op jit(solution)/shard_map/all_gather | solution.py:38
  220.1 285.1 %all-gather.21.cloned.1.call-start = ((), (), s32[]{:S(2)}) async-start(), calls=%async_computation.18 | async-start | bytes 5242880 | tf_op jit(solution)/shard_map/all_gather | solution.py:38
  220.8 339.7 %all-gather.23.cloned.1.call-start = ((), (), s32[]{:S(2)}) async-start(), calls=%async_computation.20 | async-start | bytes 9437184 | tf_op jit(solution)/shard_map/all_gather | solution.py:38
  222.1 447.0 %reduce-scatter.9.cloned.1.call-start = ((), (), s32[]{:S(2)}) async-start(), calls=%async_computation.19 | async-start | bytes 9437184 | tf_op jit(solution)/shard_map/reduce_scatter | solution.py:42
  597.7 146.4 %reduce-scatter.11.cloned.1.call-start = ((), (), s32[]{:S(2)}) async-start(), calls=%async_computation.21 | async-start | bytes 9437184 | tf_op jit(solution)/shard_map/reduce_scatter | solution.py:42
  597.8 16.4 %copy-start.41 = (bf16[2048,1024]{1,0:T(8,128)(2,1)S(1)}, bf16[2048,1024]{1,0:T(8,128)(2,1)}, u32[]{:S(2)}) copy-start(bf16[2048,1024]{1,0:T(8,128)(2,1)} %all-gather.19.cloned.1.call-done) | copy-start | bytes 12582916
  630.2 338.1 %reduce-scatter.13.cloned.1.call-start = ((), (), s32[]{:S(2)}) async-start(), calls=%async_computation.22 | async-start | bytes 9437184 | tf_op jit(solution)/shard_map/reduce_scatter | solution.py:42
  755.7 19.4 %copy-start.22 = (f32[16,4,128]{2,1,0:T(4,128)S(1)}, f32[16,4,128]{2,1,0:T(4,128)}, u32[]{:S(2)}) copy-start(f32[16,4,128]{2,1,0:T(4,128)} %copy-done.21) | copy-start | bytes 98308
  755.7 19.4 %copy-start.26 = (f32[16,4,128]{2,1,0:T(4,128)S(1)}, f32[16,4,128]{2,1,0:T(4,128)}, u32[]{:S(2)}) copy-start(f32[16,4,128]{2,1,0:T(4,128)} %copy-done.25) | copy-start | bytes 98308
  755.7 19.4 %copy-start.30 = (pred[128,128]{0,1:T(8,128)(4,1)S(1)}, pred[128,128]{0,1:T(8,128)(4,1)}, u32[]{:S(2)}) copy-start(pred[128,128]{0,1:T(8,128)(4,1)} %copy-done.29) | copy-start | bytes 49156
  897.8 149.6 %reduce-scatter.23.cloned.1.call-start = ((), (), s32[]{:S(2)}) async-start(), calls=%async_computation.27 | async-start | bytes 5242880 | tf_op jit(solution)/shard_map/reduce_scatter | solution.py:42
  912.1 214.8 %reduce-scatter.21.cloned.1.call-start = ((), (), s32[]{:S(2)}) async-start(), calls=%async_computation.26 | async-start | bytes 5242880 | tf_op jit(solution)/shard_map/reduce_scatter | solution.py:42
  926.5 280.0 %reduce-scatter.19.cloned.1.call-start = ((), (), s32[]{:S(2)}) async-start(), calls=%async_computation.25 | async-start | bytes 5242880 | tf_op jit(solution)/shard_map/reduce_scatter | solution.py:42
  941.1 313.0 %reduce-scatter.15.cloned.1.call-start = ((), (), s32[]{:S(2)}) async-start(), calls=%async_computation.23 | async-start | bytes 2621440 | tf_op jit(solution)/shard_map/reduce_scatter | solution.py:42
  942.5 25.9 %copy-start.8 = (bf16[256,2048]{1,0:T(8,128)(2,1)S(1)}, bf16[256,2048]{1,0:T(8,128)(2,1)}, u32[]{:S(2)}) copy-start(bf16[256,2048]{1,0:T(8,128)(2,1)} %param.13) | copy-start | bytes 3145732
  951.1 22.5 %copy-start.6 = (f32[256,2048]{1,0:T(8,128)S(1)}, f32[256,2048]{1,0:T(8,128)}, u32[]{:S(2)}) copy-start(f32[256,2048]{1,0:T(8,128)} %copy-done.5) | copy-start | bytes 6291460
  973.3 430.7 %reduce-scatter.17.cloned.1.call-start = ((), (), s32[]{:S(2)}) async-start(), calls=%async_computation.24 | async-start | bytes 8650752 | tf_op jit(solution)/shard_map/reduce_scatter | solution.py:42
  1256.1 149.7 %all-to-all-start.3 = ((bf16[8,64,512]{2,1,0:T(8,128)(2,1)}), bf16[8,64,512]{2,1,0:T(8,128)(2,1)}, u32[]{:S(2)}, u32[]{:S(2)}) async-start(bf16[8,64,512]{2,1,0:T(8,128)(2,1)} %bitcast.303), calls=%async_computation.7 | async-start | bytes 1048576 | tf_op jit(solution)/shard_map/all_to_all | solution.py:220
  (27 other events, 126.8 us)
Sparse Core Ops, SparseCore 0:
  26.3 45.2 all-gather.10
  73.5 53.1 all-gather.8
  129.6 77.4 all-gather.12
  208.5 79.1 all-gather.18
  290.0 52.5 all-gather.14
  344.0 80.5 all-gather.16
  426.2 78.9 all-gather.20
  507.6 52.9 all-gather.22
  597.8 71.2 reduce-scatter.8
  672.8 71.2 reduce-scatter.10
  897.9 70.3 reduce-scatter.12
  970.6 76.7 reduce-scatter.22
  1049.6 77.2 reduce-scatter.20
  1129.2 77.2 reduce-scatter.18
  1208.6 45.3 reduce-scatter.14
  1256.3 147.6 reduce-scatter.16
where the time goes:
time: 1430 us; the launch traced here: 1420 us
  waiting for transfers between devices  899 us (63%)
  matrix products  285 us (20%)
  blocking collectives  95.7 us (7%)
  other arithmetic  87.5 us (6%)
  local copies, waits for them, and re-layouts  29.8 us (2%)
  between operations  15.2 us (1%)
    reduce_scatter x8, waiting for transfers between devices, scatter(): return lax.psum_scatter(values, axes, scatter_dimension=axis, tiled=True)  490 us
    all_gather x8, waiting for transfers between devices, gather(): return lax.all_gather(values, axes, axis=axis, tiled=True)  405 us
    dot_general x5, matrix products, over_cols(): lax.dot_general(left, right, (((1,), (1,)), ((), ())), preferred_element_...  70.8 us
    dot_general x5, matrix products, over_rows(): lax.dot_general(left, right, (((0,), (0,)), ((), ())), preferred_element_...  58.6 us
    dot_general x5, matrix products, matmul(): return jnp.dot(left, right, preferred_element_type=F32)  56.9 us
    psum x1, blocking collectives, on_device(): totals = lax.psum(squares, EVERY)  44.4 us
    another operation x3, other arithmetic  33.2 us
  transfers between devices with their start and end apart: 17, of which 14 were waited for; matrix products, arithmetic and copies ran while one was open for 15% of the time, Pallas kernels for 0%

commit v1 on v0

--- a/solution.py
+++ b/solution.py
@@ -237,7 +237,7 @@
             jnp.sum(scaled_mlp * scaled_mlp),
         ]
     )
-    totals = lax.psum(squares, EVERY)
+    totals = lax.psum(lax.psum(squares, ("chip", "core")), "grp")
     rms_stats = jnp.sqrt(totals / (rows * grps * devs * D))
     return (
         layer_out.astype(BF16),

time: 1430 us -> 1430 us (level)
  blocking collectives: 95.7 us -> 76.3 us
  waiting for transfers between devices: 899 us -> 917 us
    psum x1 -> x2, blocking collectives: 44.4 us -> 25 us  [on_device(): totals = lax.psum(lax.psum(squares, ('chip', 'core')), 'grp')]
    reduce_scatter x8, waiting for transfers between devices: 490 us -> 509 us  [scatter(): return lax.psum_scatter(values, axes, scatter_dimension=axis, tiled=True)]
  transfers between devices with their start and end apart: 17 -> 17, of which waited for: 14 -> 15; matrix products, arithmetic and copies ran while one was open for 15% -> 16% of each run, Pallas kernels for 0% -> 0%
where the time goes in v1:
time: 1430 us; the launch traced here: 1420 us
  waiting for transfers between devices  917 us (64%)
  matrix products  285 us (20%)
  other arithmetic  87.3 us (6%)
  blocking collectives  76.3 us (5%)
  local copies, waits for them, and re-layouts  30.2 us (2%)
  between operations  15.1 us (1%)
    reduce_scatter x8, waiting for transfers between devices, scatter(): return lax.psum_scatter(values, axes, scatter_dimension=axis, tiled=True)  509 us
    all_gather x8, waiting for transfers between devices, gather(): return lax.all_gather(values, axes, axis=axis, tiled=True)  405 us
    dot_general x5, matrix products, over_cols(): lax.dot_general(left, right, (((1,), (1,)), ((), ())), preferred_element_...  70.9 us
    dot_general x5, matrix products, over_rows(): lax.dot_general(left, right, (((0,), (0,)), ((), ())), preferred_element_...  58.7 us
    dot_general x5, matrix products, matmul(): return jnp.dot(left, right, preferred_element_type=F32)  56.7 us
    another operation x3, other arithmetic  33 us
  transfers between devices with their start and end apart: 17, of which 15 were waited for; matrix products, arithmetic and copies ran while one was open for 16% of the time, Pallas kernels for 0%

profile of v1, /device:TPU:0, one launch (start us, length us, event | category | flops | bytes accessed | tf_op | source)
XLA Modules:
  0.0 1416.5 jit_solution(10884366551526619123)
XLA Ops:
  11.4 14.8 %all_to_all.55 = bf16[64,8,512]{2,0,1:T(8,128)(2,1)} all-to-all(bf16[64,8,512]{2,0,1:T(8,128)(2,1)S(1)} %copy.186), channel_id=1, replica_groups=mesh['grp'=4,'chip'=4,'core'=2] {'chip','core'}, dimensions={1} | all-to-all | bytes 1048576 | tf_op jit(solution)/shard_map/all_to_all | solution.py:101
  28.9 42.7 %all-gather.11.cloned.1.call-done = bf16[2048,512]{1,0:T(8,128)(2,1)} async-done(((bf16[512,512]{1,0:T(8,128)(2,1)}), bf16[2048,512]{1,0:T(8,128)(2,1)}) %all-gather.11.cloned.1.call-update) | async-done | bytes 2097168 | tf_op jit(solution)/shard_map/all_gather | solution.py:38
  73.5 53.2 %all-gather.9.cloned.1.call-done = bf16[2048,2048]{1,0:T(8,128)(2,1)} async-done(((bf16[256,2048]{1,0:T(8,128)(2,1)}), bf16[2048,2048]{1,0:T(8,128)(2,1)}) %all-gather.9.cloned.1.call-update) | async-done | bytes 8388624 | tf_op jit(solution)/shard_map/all_gather | solution.py:38
  174.2 15.8 %fusion.42 = bf16[1,16,128,1,4,64]{2,5,4,1,3,0:T(8,128)(2,1)S(1)} fusion(f32[16,64,4,128]{3,1,2,0:T(8,128)S(1)} %fusion.45, bf16[1,2048,1,64]{1,3,2,0:T(8,128)(2,1)S(1)} %bitcast.311, f32[16,4,128]{2,1,0:T(4,128)S(1)} %add.140, f32[16,4,128]{2,1,0:T(4,128)S(1)} %max.8, f32[1024,16,128,4]{2,0,3,1:T(8,128)} %copy-done, ...), kind=kOutput, calls=%fused_computation.82 | convolution fusion | flops 1116733440 | bytes 36913152 | tf_op jit(solution)/shard_map/gbkpij,gjkd->gbikpd/dot_general | solution.py:139
  191.2 18.5 %all_to_all.56 = bf16[8,256,256]{2,1,0:T(8,128)(2,1)S(1)} all-to-all(bf16[8,256,256]{2,1,0:T(8,128)(2,1)S(1)} %bitcast.291), channel_id=1, replica_groups=mesh['grp'=4,'chip'=4,'core'=2] {'chip','core'}, dimensions={0} | all-to-all | bytes 2097152 | tf_op jit(solution)/shard_map/all_to_all | solution.py:143
  222.6 65.1 %all-gather.19.cloned.1.call-done = bf16[2048,1024]{1,0:T(8,128)(2,1)} async-done(((bf16[2048,256]{1,0:T(8,128)(2,1)}), bf16[2048,1024]{1,0:T(8,128)(2,1)}) %all-gather.19.cloned.1.call-update) | async-done | bytes 4194320 | tf_op jit(solution)/shard_map/all_gather | solution.py:38
  287.7 54.9 %all-gather.15.cloned.1.call-done = bf16[2048,2048]{1,0:T(8,128)(2,1)} async-done(((bf16[256,2048]{1,0:T(8,128)(2,1)}), bf16[2048,2048]{1,0:T(8,128)(2,1)}) %all-gather.15.cloned.1.call-update) | async-done | bytes 8388624 | tf_op jit(solution)/shard_map/all_gather | solution.py:38
  342.6 14.5 %fusion.94 = f32[2048,1024]{1,0:T(8,128)} fusion(bf16[2048,2048]{1,0:T(8,128)(2,1)} %all-gather.15.cloned.1.call-done, bf16[2048,1024]{1,0:T(8,128)(2,1)} %all-gather.19.cloned.1.call-done), kind=kOutput, calls=%fused_computation.166 | convolution fusion | flops 8589934592 | bytes 20971520 | tf_op jit(solution)/shard_map/dot_general | solution.py:26
  357.1 67.5 %all-gather.17.cloned.1.call-done = bf16[2048,1024]{1,0:T(8,128)(2,1)} async-done(((bf16[2048,256]{1,0:T(8,128)(2,1)}), bf16[2048,1024]{1,0:T(8,128)(2,1)}) %all-gather.17.cloned.1.call-update) | async-done | bytes 4194320 | tf_op jit(solution)/shard_map/all_gather | solution.py:38
  424.6 14.4 %fusion.93 = f32[2048,1024]{1,0:T(8,128)} fusion(bf16[2048,2048]{1,0:T(8,128)(2,1)} %all-gather.15.cloned.1.call-done, bf16[2048,1024]{1,0:T(8,128)(2,1)} %all-gather.17.cloned.1.call-done), kind=kOutput, calls=%fused_computation.165 | convolution fusion | flops 8589934592 | bytes 20971520 | tf_op jit(solution)/shard_map/dot_general | solution.py:26
  439.0 66.1 %all-gather.21.cloned.1.call-done = bf16[1024,2048]{1,0:T(8,128)(2,1)} async-done(((bf16[256,2048]{1,0:T(8,128)(2,1)}), bf16[1024,2048]{1,0:T(8,128)(2,1)}) %all-gather.21.cloned.1.call-update) | async-done | bytes 4194320 | tf_op jit(solution)/shard_map/all_gather | solution.py:38
  505.2 55.4 %all-gather.23.cloned.1.call-done = bf16[2048,2048]{1,0:T(8,128)(2,1)} async-done(((bf16[256,2048]{1,0:T(8,128)(2,1)}), bf16[2048,2048]{1,0:T(8,128)(2,1)}) %all-gather.23.cloned.1.call-update) | async-done | bytes 8388624 | tf_op jit(solution)/shard_map/all_gather | solution.py:38
  560.6 23.2 %multiply_convert_fusion = (bf16[2048,1024]{1,0:T(8,128)(2,1)}, bf16[2048,1024]{1,0:T(8,128)(2,1)}, bf16[2048,1024]{1,0:T(8,128)(2,1)}) fusion(f32[2048,1024]{1,0:T(8,128)} %fusion.93, f32[2048,1024]{1,0:T(8,128)} %fusion.94, bf16[2048,2048]{1,0:T(8,128)(2,1)} %all-gather.23.cloned.1.call-done, bf16[1024,2048]{1,0:T(8,128)(2,1)} %all-gather.21.cloned.1.call-done), kind=kOutput, calls=%fused_computation.26 | convolution fusion | flops 8621391872 | bytes 41943040 | tf_op jit(solution)/shard_map/dot_general | solution.py:34
  583.7 13.9 convolution_convert_fusion.2
  597.8 16.5 %fusion.95 = f32[2048,2048]{1,0:T(8,128)} fusion(bf16[2048,1024]{1,0:T(8,128)(2,1)} %get-tuple-element.24, bf16[2048,1024]{1,0:T(8,128)(2,1)} %all-gather.17.cloned.1.call-done), kind=kOutput, calls=%fused_computation.167 | convolution fusion | flops 8589934592 | bytes 25165824 | tf_op jit(solution)/shard_map/dot_general | solution.py:34
  614.3 16.0 %add_convert_fusion = bf16[2048,2048]{1,0:T(8,128)(2,1)} fusion(f32[2048,2048]{1,0:T(8,128)} %fusion.95, bf16[2048,1024]{1,0:T(8,128)(2,1)} %get-tuple-element.23, bf16[2048,1024]{1,0:T(8,128)(2,1)S(1)} %copy-done.41), kind=kOutput, calls=%fused_computation.24 | convolution fusion | flops 8598323200 | bytes 33554432 | tf_op jit(solution)/shard_map/dot_general | solution.py:34
  630.5 38.6 %reduce-scatter.9.cloned.1.call-done = bf16[256,2048]{1,0:T(8,128)(2,1)} async-done(((bf16[2048,2048]{1,0:T(8,128)(2,1)}), bf16[256,2048]{1,0:T(8,128)(2,1)}) %reduce-scatter.9.cloned.1.call-update) | async-done | bytes 1048592 | tf_op jit(solution)/shard_map/reduce_scatter | solution.py:42
  669.1 75.0 %reduce-scatter.11.cloned.1.call-done = bf16[256,2048]{1,0:T(8,128)(2,1)} async-done(((bf16[2048,2048]{1,0:T(8,128)(2,1)}), bf16[256,2048]{1,0:T(8,128)(2,1)}) %reduce-scatter.11.cloned.1.call-update) | async-done | bytes 1048592 | tf_op jit(solution)/shard_map/reduce_scatter | solution.py:42
  755.8 17.9 %all_to_all.57 = bf16[256,8,256]{2,0,1:T(8,128)(2,1)S(1)} all-to-all(bf16[256,8,256]{2,0,1:T(8,128)(2,1)S(1)} %bitcast.293), channel_id=1, replica_groups=mesh['grp'=4,'chip'=4,'core'=2] {'chip','core'}, dimensions={1} | all-to-all | bytes 2097152 | tf_op jit(solution)/shard_map/all_to_all | solution.py:177
  782.6 26.2 %fusion = (f32[16,4,128]{2,1,0:T(4,128)S(1)}, f32[1024,16,128,4]{2,0,3,1:T(8,128)}) fusion(f32[16,4,128]{2,1,0:T(4,128)S(1)} %copy-done.26, f32[16,4,128]{2,1,0:T(4,128)S(1)} %copy-done.22, f32[1024,16,128,4]{2,0,3,1:T(8,128)} %copy-done, pred[16,1024]{1,0:T(8,128)(4,1)S(1)} %copy-done.24, bf16[16,128,4,64]{1,3,2,0:T(8,128)(2,1)S(1)} %bitcast.316, ...), kind=kOutput, calls=%fused_computation.7 | convolution fusion | flops 1124065280 | bytes 68403200 | tf_op jit(solution)/shard_map/gbikpd,gjkd->gbkpij/dot_general | solution.py:180
  808.9 14.7 %fusion.65 = bf16[1,1024,64]{1,2,0:T(8,128)(2,1)S(1)} fusion(bf16[16,128,4,64]{1,3,2,0:T(8,128)(2,1)S(1)} %bitcast.317, f32[1,1024,64]{1,0,2:T(1,128)S(1)} %slice.91, f32[16,4,128]{2,1,0:T(4,128)S(1)} %copy-done.26, f32[16,4,128]{2,1,0:T(4,128)S(1)} %copy-done.22, f32[1024,16,128,4]{2,0,3,1:T(8,128)} %copy-done, pred[16,1024]{1,0:T(8,128)(4,1)S(1)} %copy-done.24), kind=kOutput, calls=%fused_computation.107 | convolution fusion | flops 1115815936 | bytes 35078144 | tf_op jit(solution)/shard_map/gbkpij,gbikpd->gjkd/dot_general | solution.py:193
  823.9 27.9 %fusion.9 = bf16[16,4,128,1024]{2,3,1,0:T(8,128)(2,1)} fusion(f32[1024,16,128,4]{2,0,3,1:T(8,128)} %get-tuple-element.41, f32[16,4,128]{2,1,0:T(4,128)S(1)} %add.151, f32[16,4,128]{2,1,0:T(4,128)S(1)} %copy-done.26, f32[16,4,128]{2,1,0:T(4,128)S(1)} %copy-done.22, f32[1024,16,128,4]{2,0,3,1:T(8,128)} %copy-done, pred[16,1024]{1,0:T(8,128)(4,1)S(1)} %copy-done.24), kind=kLoop, calls=%fused_computation.19 | loop fusion | flops 58720256 | bytes 84000768 | tf_op jit(solution)/shard_map/reshape.53
  897.7 14.5 %convolution_convert_fusion.3 = bf16[1024,2048]{1,0:T(8,128)(2,1)} fusion(bf16[2048,1024]{1,0:T(8,128)(2,1)} %get-tuple-element.25, bf16[2048,2048]{1,0:T(8,128)(2,1)} %all-gather.23.cloned.1.call-done), kind=kOutput, calls=%fused_computation.46 | convolution fusion | flops 8592031744 | bytes 16777216 | tf_op jit(solution)/shard_map/dot_general | solution.py:30
  912.2 14.2 %convolution_convert_fusion.4 = bf16[2048,1024]{1,0:T(8,128)(2,1)} fusion(bf16[2048,2048]{1,0:T(8,128)(2,1)} %all-gather.15.cloned.1.call-done, bf16[2048,1024]{1,0:T(8,128)(2,1)} %get-tuple-element.23), kind=kOutput, calls=%fused_computation.47 | convolution fusion | flops 8592031744 | bytes 16777216 | tf_op jit(solution)/shard_map/dot_general | solution.py:30
  926.5 14.5 %convolution_convert_fusion.5 = bf16[2048,1024]{1,0:T(8,128)(2,1)} fusion(bf16[2048,2048]{1,0:T(8,128)(2,1)} %all-gather.15.cloned.1.call-done, bf16[2048,1024]{1,0:T(8,128)(2,1)} %get-tuple-element.24), kind=kOutput, calls=%fused_computation.48 | convolution fusion | flops 8592031744 | bytes 16777216 | tf_op jit(solution)/shard_map/dot_general | solution.py:30
  951.1 17.0 %reduce-scatter.13.cloned.1.call-done = bf16[256,2048]{1,0:T(8,128)(2,1)} async-done(((bf16[2048,2048]{1,0:T(8,128)(2,1)}), bf16[256,2048]{1,0:T(8,128)(2,1)}) %reduce-scatter.13.cloned.1.call-update) | async-done | bytes 1048592 | tf_op jit(solution)/shard_map/reduce_scatter | solution.py:42
  980.2 67.0 %reduce-scatter.23.cloned.1.call-done = bf16[256,2048]{1,0:T(8,128)(2,1)} async-done(((bf16[1024,2048]{1,0:T(8,128)(2,1)}), bf16[256,2048]{1,0:T(8,128)(2,1)}) %reduce-scatter.23.cloned.1.call-update) | async-done | bytes 1048592 | tf_op jit(solution)/shard_map/reduce_scatter | solution.py:42
  1052.0 74.8 %reduce-scatter.21.cloned.1.call-done = bf16[2048,256]{1,0:T(8,128)(2,1)} async-done(((bf16[2048,1024]{1,0:T(8,128)(2,1)}), bf16[2048,256]{1,0:T(8,128)(2,1)}) %reduce-scatter.21.cloned.1.call-update) | async-done | bytes 1048592 | tf_op jit(solution)/shard_map/reduce_scatter | solution.py:42
  1129.5 14.0 psum.14
  1143.5 62.8 %reduce-scatter.19.cloned.1.call-done = bf16[2048,256]{1,0:T(8,128)(2,1)} async-done(((bf16[2048,1024]{1,0:T(8,128)(2,1)}), bf16[2048,256]{1,0:T(8,128)(2,1)}) %reduce-scatter.19.cloned.1.call-update) | async-done | bytes 1048592 | tf_op jit(solution)/shard_map/reduce_scatter | solution.py:42
  1220.6 32.4 %reduce-scatter.15.cloned.1.call-done = bf16[512,512]{0,1:T(8,128)(2,1)} async-done(((bf16[2048,512]{0,1:T(8,128)(2,1)}), bf16[512,512]{0,1:T(8,128)(2,1)}) %reduce-scatter.15.cloned.1.call-update) | async-done | bytes 524304 | tf_op jit(solution)/shard_map/reduce_scatter | solution.py:42
  1261.9 141.3 %reduce-scatter.17.cloned.1.call-done = bf16[64,2048]{1,0:T(8,128)(2,1)} async-done(((bf16[2048,2048]{1,0:T(8,128)(2,1)}), bf16[64,2048]{1,0:T(8,128)(2,1)}) %reduce-scatter.17.cloned.1.call-update) | async-done | bytes 262160 | tf_op jit(solution)/shard_map/reduce_scatter | solution.py:42
  (223 shorter events, 196.0 us)
Async XLA Ops:
  7.2 21.2 %copy-start.39 = (s32[64]{0:T(128)S(1)}, s32[64]{0:T(128)}, u32[]{:S(2)}) copy-start(s32[64]{0:T(128)} %param.15) | copy-start | bytes 772
  7.2 21.2 %copy-start.40 = (s32[64]{0:T(128)S(1)}, s32[64]{0:T(128)}, u32[]{:S(2)}) copy-start(s32[64]{0:T(128)} %param.14) | copy-start | bytes 772
  7.2 64.5 %all-gather.11.cloned.1.call-start = ((), (), s32[]{:S(2)}) async-start(), calls=%async_computation.13 | async-start | bytes 2621440 | tf_op jit(solution)/shard_map/all_gather | solution.py:38
  26.2 100.5 %all-gather.9.cloned.1.call-start = ((), (), s32[]{:S(2)}) async-start(), calls=%async_computation.12 | async-start | bytes 9437184 | tf_op jit(solution)/shard_map/all_gather | solution.py:38
  27.0 184.1 %all-gather.13.cloned.1.call-start = ((), (), s32[]{:S(2)}) async-start(), calls=%async_computation.14 | async-start | bytes 8650752 | tf_op jit(solution)/shard_map/all_gather | solution.py:38
  27.7 260.0 %all-gather.19.cloned.1.call-start = ((), (), s32[]{:S(2)}) async-start(), calls=%async_computation.17 | async-start | bytes 5242880 | tf_op jit(solution)/shard_map/all_gather | solution.py:38
  28.3 314.3 %all-gather.15.cloned.1.call-start = ((), (), s32[]{:S(2)}) async-start(), calls=%async_computation.15 | async-start | bytes 9437184 | tf_op jit(solution)/shard_map/all_gather | solution.py:38
  28.8 144.2 %copy-start.29 = (pred[128,128]{0,1:T(8,128)(4,1)}, pred[128,128]{0,1:T(8,128)(4,1)S(1)}, u32[]{:S(2)}) copy-start(pred[128,128]{0,1:T(8,128)(4,1)S(1)} %iota_compare_fusion.1) | copy-start | bytes 49156
  28.8 109.9 %copy-start.38 = (s32[1024]{0:T(1024)}, s32[1024]{0:T(1024)S(1)}, u32[]{:S(2)}) copy-start(s32[1024]{0:T(1024)S(1)} %pad_clamp_fusion.1) | copy-start | bytes 12292
  28.8 161.8 %copy-start.37 = (s32[1024]{0:T(1024)}, s32[1024]{0:T(1024)S(1)}, u32[]{:S(2)}) copy-start(s32[1024]{0:T(1024)S(1)} %pad_clamp_fusion) | copy-start | bytes 12292
  28.9 145.3 %copy-start.23 = (pred[16,1024]{1,0:T(8,128)(4,1)}, pred[16,1024]{1,0:T(8,128)(4,1)S(1)}, u32[]{:S(2)}) copy-start(pred[16,1024]{1,0:T(8,128)(4,1)S(1)} %iota_compare_fusion.2) | copy-start | bytes 49156
  73.5 58.5 %copy-start.31 = (f32[2048]{0:T(1024)}, f32[2048]{0:T(1024)S(1)}, u32[]{:S(2)}) copy-start(f32[2048]{0:T(1024)S(1)} %get-tuple-element.18) | copy-start | bytes 24580
  157.1 17.1 %copy-start.21 = (f32[16,4,128]{2,1,0:T(4,128)}, f32[16,4,128]{2,1,0:T(4,128)S(1)}, u32[]{:S(2)}) copy-start(f32[16,4,128]{2,1,0:T(4,128)S(1)} %max.8) | copy-start | bytes 98308
  190.0 21.0 %copy-start.7 = (bf16[256,2048]{1,0:T(8,128)(2,1)S(1)}, bf16[256,2048]{1,0:T(8,128)(2,1)}, u32[]{:S(2)}) copy-start(bf16[256,2048]{1,0:T(8,128)(2,1)} %param.13) | copy-start | bytes 3145732
  219.9 204.7 %all-gather.17.cloned.1.call-start = ((), (), s32[]{:S(2)}) async-start(), calls=%async_computation.16 | async-start | bytes 5242880 | tf_op jit(solution)/shard_map/all_gather | solution.py:38
  220.5 284.6 %all-gather.21.cloned.1.call-start = ((), (), s32[]{:S(2)}) async-start(), calls=%async_computation.18 | async-start | bytes 5242880 | tf_op jit(solution)/shard_map/all_gather | solution.py:38
  221.3 339.3 %all-gather.23.cloned.1.call-start = ((), (), s32[]{:S(2)}) async-start(), calls=%async_computation.20 | async-start | bytes 9437184 | tf_op jit(solution)/shard_map/all_gather | solution.py:38
  222.5 446.6 %reduce-scatter.9.cloned.1.call-start = ((), (), s32[]{:S(2)}) async-start(), calls=%async_computation.19 | async-start | bytes 9437184 | tf_op jit(solution)/shard_map/reduce_scatter | solution.py:42
  597.7 146.5 %reduce-scatter.11.cloned.1.call-start = ((), (), s32[]{:S(2)}) async-start(), calls=%async_computation.21 | async-start | bytes 9437184 | tf_op jit(solution)/shard_map/reduce_scatter | solution.py:42
  597.7 16.5 %copy-start.41 = (bf16[2048,1024]{1,0:T(8,128)(2,1)S(1)}, bf16[2048,1024]{1,0:T(8,128)(2,1)}, u32[]{:S(2)}) copy-start(bf16[2048,1024]{1,0:T(8,128)(2,1)} %all-gather.19.cloned.1.call-done) | copy-start | bytes 12582916
  630.3 337.8 %reduce-scatter.13.cloned.1.call-start = ((), (), s32[]{:S(2)}) async-start(), calls=%async_computation.22 | async-start | bytes 9437184 | tf_op jit(solution)/shard_map/reduce_scatter | solution.py:42
  755.7 19.4 %copy-start.22 = (f32[16,4,128]{2,1,0:T(4,128)S(1)}, f32[16,4,128]{2,1,0:T(4,128)}, u32[]{:S(2)}) copy-start(f32[16,4,128]{2,1,0:T(4,128)} %copy-done.21) | copy-start | bytes 98308
  755.7 19.4 %copy-start.26 = (f32[16,4,128]{2,1,0:T(4,128)S(1)}, f32[16,4,128]{2,1,0:T(4,128)}, u32[]{:S(2)}) copy-start(f32[16,4,128]{2,1,0:T(4,128)} %copy-done.25) | copy-start | bytes 98308
  755.7 19.4 %copy-start.30 = (pred[128,128]{0,1:T(8,128)(4,1)S(1)}, pred[128,128]{0,1:T(8,128)(4,1)}, u32[]{:S(2)}) copy-start(pred[128,128]{0,1:T(8,128)(4,1)} %copy-done.29) | copy-start | bytes 49156
  897.6 149.6 %reduce-scatter.23.cloned.1.call-start = ((), (), s32[]{:S(2)}) async-start(), calls=%async_computation.27 | async-start | bytes 5242880 | tf_op jit(solution)/shard_map/reduce_scatter | solution.py:42
  912.2 214.6 %reduce-scatter.21.cloned.1.call-start = ((), (), s32[]{:S(2)}) async-start(), calls=%async_computation.26 | async-start | bytes 5242880 | tf_op jit(solution)/shard_map/reduce_scatter | solution.py:42
  926.5 279.8 %reduce-scatter.19.cloned.1.call-start = ((), (), s32[]{:S(2)}) async-start(), calls=%async_computation.25 | async-start | bytes 5242880 | tf_op jit(solution)/shard_map/reduce_scatter | solution.py:42
  941.1 311.9 %reduce-scatter.15.cloned.1.call-start = ((), (), s32[]{:S(2)}) async-start(), calls=%async_computation.23 | async-start | bytes 2621440 | tf_op jit(solution)/shard_map/reduce_scatter | solution.py:42
  942.4 25.7 %copy-start.8 = (bf16[256,2048]{1,0:T(8,128)(2,1)S(1)}, bf16[256,2048]{1,0:T(8,128)(2,1)}, u32[]{:S(2)}) copy-start(bf16[256,2048]{1,0:T(8,128)(2,1)} %param.13) | copy-start | bytes 3145732
  951.1 22.2 %copy-start.6 = (f32[256,2048]{1,0:T(8,128)S(1)}, f32[256,2048]{1,0:T(8,128)}, u32[]{:S(2)}) copy-start(f32[256,2048]{1,0:T(8,128)} %copy-done.5) | copy-start | bytes 6291460
  973.1 430.1 %reduce-scatter.17.cloned.1.call-start = ((), (), s32[]{:S(2)}) async-start(), calls=%async_computation.24 | async-start | bytes 8650752 | tf_op jit(solution)/shard_map/reduce_scatter | solution.py:42
  1255.0 150.0 %all-to-all-start.3 = ((bf16[8,64,512]{2,1,0:T(8,128)(2,1)}), bf16[8,64,512]{2,1,0:T(8,128)(2,1)}, u32[]{:S(2)}, u32[]{:S(2)}) async-start(bf16[8,64,512]{2,1,0:T(8,128)(2,1)} %bitcast.303), calls=%async_computation.7 | async-start | bytes 1048576 | tf_op jit(solution)/shard_map/all_to_all | solution.py:220
  (27 other events, 126.7 us)
Sparse Core Ops, SparseCore 0:
  26.3 45.2 all-gather.10
  73.5 53.1 all-gather.8
  129.6 77.4 all-gather.12
  208.5 79.1 all-gather.18
  290.0 52.5 all-gather.14
  344.0 80.5 all-gather.16
  426.2 78.9 all-gather.20
  507.6 52.9 all-gather.22
  597.8 71.2 reduce-scatter.8
  672.8 71.2 reduce-scatter.10
  897.7 70.3 reduce-scatter.12
  970.4 76.7 reduce-scatter.22
  1049.5 77.2 reduce-scatter.20
  1129.0 77.2 reduce-scatter.18
  1208.5 44.4 reduce-scatter.14
  1255.2 147.9 reduce-scatter.16
